TPU v7x, 512 devices: a whole 4x4x16 slice. The times are simulated.
512 devices in a mesh: dp: 32 (over x_hi, z), spatial: 16 (over x_lo, y, core).
Axes of the slice: x: 4 (x_hi: 2, x_lo: 2; x = x_hi * 2 + x_lo), y: 4, z: 16, core: 2. Of those that a mesh axis runs over, the one named last changes fastest.
Arguments:
- latents: bfloat16 [64, 32, 32, 640], P('dp', 'spatial'), may hold values from -16 to 16
- plan: bfloat16 [64, 256, 640], P('dp', 'spatial'), may hold values from -45 to 45
- conv_weight: bfloat16 [9, 640, 640], P(None, 'dp'), may hold values from -0.078125 to 0.078125
- gn_gain: float32 [640], replicated, may hold values from 0.5 to 2
- attn_weights: bfloat16 [4, 640, 640], P(None, 'dp'), may hold values from -0.25 to 0.25
- cotangent: bfloat16 [64, 32, 32, 640], P('dp', 'spatial'), may hold values from -6 to 6
Outputs:
- block_out: bfloat16 [64, 32, 32, 640], P('dp', 'spatial')
- weight_grads: float32 [640, 2, 640], P('dp')
All inputs are finite; a program needn't handle non-finite values.
Results may differ from a plain program's by a relative error of at most 0.03.
The roundings to bfloat16 on the way count: a program that leaves them out, or rounds other values in their place, can miss the bound.
Values may be sent and summed in bfloat16 or wider, within the bound.
A program may use at most 64 MiB of HBM per device.

v0:
```python
import math
import jax
import jax.numpy as jnp
from jax import lax
from jax.sharding import PartitionSpec as P

GROUPS = 32
HEAD = 64
eps_norm = 1e-05


def with_halo(cells, sides, width):
    for axis, dim in sides:
        count = lax.axis_size(axis)
        ends = count - 1
        head = lax.slice_in_dim(cells, 0, width, axis=dim)
        tail = lax.slice_in_dim(cells, cells.shape[dim] - width, cells.shape[dim], axis=dim)
        cells = jnp.concatenate(
            [
                lax.ppermute(tail, axis, [(i, (i + 1) % count) for i in range(ends)]),
                cells,
                lax.ppermute(head, axis, [((i + 1) % count, i) for i in range(ends)]),
            ],
            axis=dim,
        )
    return cells


def body(latents, plan, conv_weight, gn_gain, attn_weights, cotangent):
    images, band_rows, columns, channels = latents.shape
    heads = channels // HEAD
    per_group = channels // GROUPS
    tokens_here = images * band_rows * columns
    scale = 1.0 / math.sqrt(HEAD)
    flat_input = latents.astype(jnp.float32).reshape(images, band_rows * columns, GROUPS, per_group)
    first_sums = jnp.sum(flat_input, axis=(1, 3))
    second_sums = jnp.sum(flat_input * flat_input, axis=(1, 3))
    first_sums, second_sums = lax.psum((first_sums, second_sums), "spatial")
    counted = float(band_rows * lax.axis_size("spatial") * columns * per_group)
    means = first_sums / counted
    variance = second_sums / counted - means * means
    inverse = lax.rsqrt(variance + eps_norm)
    normed = (flat_input - means[:, None, :, None]) * inverse[:, None, :, None]
    normed = normed.reshape(images, band_rows, columns, channels) * gn_gain
    hidden = jax.nn.silu(normed).astype(jnp.bfloat16)
    padded = with_halo(hidden, (("spatial", 1),), 1)
    padded = jnp.pad(padded, ((0, 0), (0, 0), (1, 1), (0, 0)))
    tapped = jnp.stack(
        [
            padded[:, offset_y : offset_y + band_rows, offset_x : offset_x + columns].reshape(
                tokens_here, channels
            )
            for offset_y in range(3)
            for offset_x in range(3)
        ],
        1,
    )
    conv_sum = jnp.einsum(
        "ntc,tcd->nd",
        tapped,
        lax.all_gather(conv_weight, "dp", axis=1, tiled=True),
        preferred_element_type=jnp.float32,
    )
    mixed = (latents.reshape(tokens_here, channels).astype(jnp.float32) + conv_sum).astype(
        jnp.bfloat16
    )
    weights = lax.all_gather(attn_weights, "dp", axis=1, tiled=True)
    weight_q = weights[0]
    weight_k = weights[1]
    weight_v = weights[2]
    weight_o = weights[3]
    queries = jnp.dot(mixed, weight_q, preferred_element_type=jnp.float32).astype(jnp.bfloat16)
    plan_all = lax.all_gather(plan, "spatial", axis=1, tiled=True)
    plan_flat = plan_all.reshape(-1, channels)
    keys_all = jnp.dot(plan_flat, weight_k, preferred_element_type=jnp.float32).astype(jnp.bfloat16)
    values_all = jnp.dot(plan_flat, weight_v, preferred_element_type=jnp.float32).astype(
        jnp.bfloat16
    )
    keys_all = keys_all.reshape(images, -1, channels)
    values_all = values_all.reshape(images, -1, channels)
    plan_tokens = keys_all.shape[1]
    query_heads = queries.reshape(images, band_rows * columns, heads, HEAD)
    key_heads = keys_all.reshape(images, plan_tokens, heads, HEAD)
    value_heads = values_all.reshape(images, plan_tokens, heads, HEAD)
    scores = (
        jnp.einsum("bnhe,bmhe->bhnm", query_heads, key_heads, preferred_element_type=jnp.float32)
        * scale
    )
    maxima = jnp.max(scores, axis=-1, keepdims=True)
    expo = jnp.exp(scores - maxima)
    probs = expo / jnp.sum(expo, axis=-1, keepdims=True)
    probs_b = probs.astype(jnp.bfloat16)
    attended = jnp.einsum(
        "bhnm,bmhe->bnhe", probs_b, value_heads, preferred_element_type=jnp.float32
    )
    attended = attended.reshape(tokens_here, channels).astype(jnp.bfloat16)
    result = mixed.astype(jnp.float32) + jnp.dot(
        attended, weight_o, preferred_element_type=jnp.float32
    )
    block_out = result.astype(jnp.bfloat16).reshape(images, band_rows, columns, channels)
    grad_flat = cotangent.reshape(tokens_here, channels)
    grad_att = lax.dot_general(
        grad_flat, weight_o, (((1,), (1,)), ((), ())), preferred_element_type=jnp.float32
    )
    grad_att = grad_att.astype(jnp.bfloat16).reshape(images, band_rows * columns, heads, HEAD)
    dprob = jnp.einsum("bnhe,bmhe->bhnm", grad_att, value_heads, preferred_element_type=jnp.float32)
    dscore = (probs * (dprob - jnp.sum(probs * dprob, axis=-1, keepdims=True)) * scale).astype(
        jnp.bfloat16
    )
    dquery = jnp.einsum("bhnm,bmhe->bnhe", dscore, key_heads, preferred_element_type=jnp.float32)
    dquery = dquery.reshape(tokens_here, channels).astype(jnp.bfloat16)
    total_tokens = images * lax.axis_size("dp") * band_rows * lax.axis_size("spatial") * columns
    factor = 1.0 / math.sqrt(total_tokens)
    contract = (((0,), (0,)), ((), ()))
    grad_query = lax.dot_general(mixed, dquery, contract, preferred_element_type=jnp.float32)
    grad_output = lax.dot_general(attended, grad_flat, contract, preferred_element_type=jnp.float32)
    own_rows = lax.psum_scatter(
        jnp.stack([grad_query, grad_output], 1) * factor, "dp", scatter_dimension=0, tiled=True
    )
    weight_grads = lax.psum(own_rows, "spatial")
    return (block_out, weight_grads)


def solution(mesh):
    return jax.shard_map(
        body,
        mesh=mesh,
        in_specs=(
            P("dp", "spatial", None, None),
            P("dp", "spatial", None),
            P(None, "dp", None),
            P(),
            P(None, "dp", None),
            P("dp", "spatial", None, None),
        ),
        out_specs=(P("dp", "spatial", None, None), P("dp", None, None)),
        check_vma=False,
    )
```

profile of v0, /device:TPU:1, one launch (start us, length us, event | category | flops | bytes accessed | tf_op | source)
XLA Modules:
  0.0 876.4 jit_solution(7868620939936180710)
XLA Ops:
  8.0 1.8 copy.29
  11.2 33.4 %all-reduce.2 = (f32[2,32]{1,0:T(2,128)S(1)}, f32[2,32]{1,0:T(2,128)S(1)}) all-reduce(f32[2,32]{1,0:T(2,128)S(1)} %reduce_sum.55, f32[2,32]{1,0:T(2,128)S(1)} %reduce_sum.52), channel_id=1, replica_groups=mesh['dp'=32,'spatial'=16] {'spatial'}, use_global_device_ids=true, to_apply=%region_5.6 | all-reduce | flops 128 | bytes 1024 | tf_op jit(solution)/shard_map/psum | solution.py:38
  45.2 1.9 collective-permute-start
  47.1 2.4 collective-permute-start.1
  49.5 19.2 %all_gather.10 = bf16[2,256,640]{2,1,0:T(8,128)(2,1)S(1)} all-gather(bf16[2,16,640]{2,1,0:T(8,128)(2,1)S(1)} %copy-done.7), channel_id=1, replica_groups=mesh['dp'=32,'spatial'=16] {'spatial'}, dimensions={1}, use_global_device_ids=true | all-gather | bytes 696320 | tf_op jit(solution)/shard_map/all_gather | solution.py:73
  75.1 89.4 %all-gather.5.cloned.1.call-done = bf16[4,640,640]{2,0,1:T(4,128)(2,1)} async-done(((bf16[4,20,640]{2,0,1:T(4,128)(2,1)}), bf16[4,640,640]{2,0,1:T(4,128)(2,1)}) %all-gather.5.cloned.1.call-update) | async-done | bytes 3276816 | tf_op jit(solution)/shard_map/all_gather | solution.py:67
  164.4 12.3 %fusion.57 = (bf16[1,640,640]{2,0,1:T(2,128)(2,1)S(1)}, bf16[1,640,640]{2,0,1:T(2,128)(2,1)S(1)}, bf16[1,640,640]{2,0,1:T(2,128)(2,1)}, bf16[1,640,640]{2,0,1:T(2,128)(2,1)}) fusion(bf16[4,640,640]{2,0,1:T(4,128)(2,1)} %all-gather.5.cloned.1.call-done), kind=kLoop, calls=%fused_computation.73 | loop fusion | bytes 6553600 | tf_op jit(solution)/shard_map/slice | solution.py:71
  176.7 1.6 convolution_convert_fusion
  180.7 2.2 convolution_convert_fusion.1
  184.0 1.4 fusion.33
  185.4 213.4 %all-gather.3.cloned.1.call-done = bf16[9,640,640]{2,0,1:T(8,128)(2,1)} async-done(((bf16[9,20,640]{2,0,1:T(8,128)(2,1)}), bf16[9,640,640]{2,0,1:T(8,128)(2,1)}) %all-gather.3.cloned.1.call-update) | async-done | bytes 7372816 | tf_op jit(solution)/shard_map/all_gather | solution.py:61
  398.8 7.7 fusion.27
  408.7 2.6 fusion.60
  411.3 2.5 fusion.19
  413.8 9.3 %fusion.20 = bf16[2,64,10,64]{1,3,2,0:T(8,128)(2,1)S(1)} fusion(f32[2,10,64,256]{3,2,1,0:T(8,128)} %fusion.33, bf16[2,256,10,64]{1,0,3,2:T(2,128)(2,1)S(1)} %copy-done.3, f32[2,10,64,256]{3,2,1,0:T(8,128)} %get-tuple-element.27, f32[2,10,64]{2,1,0:T(8,128)S(1)} %get-tuple-element.26), kind=kOutput, calls=%fused_computation.25 | convolution fusion | flops 44320256 | bytes 3445760 | tf_op jit(solution)/shard_map/bhnm,bmhe->bnhe/dot_general | solution.py:110
  424.3 1.4 convolution_bitcast_fusion.1
  425.7 2.0 copy.40
  427.7 1.8 convert_element_type.72
  431.2 4.3 copy.47
  435.6 1.3 dynamic-slice
  437.6 285.5 %all-reduce.8.cloned.1.call-done = f32[640,2,640]{2,1,0:T(2,128)} async-done(((f32[640,2,640]{2,1,0:T(2,128)}), f32[640,2,640]{2,1,0:T(2,128)}) %all-reduce.8.cloned.1.call-update) | async-done | bytes 3276816
  723.1 1.5 constant_dynamic-slice_fusion
  725.7 142.7 %all-reduce.6.cloned.1.call-done = f32[20,2,640]{2,1,0:T(2,128)} async-done(((f32[20,2,640]{2,1,0:T(2,128)}), f32[20,2,640]{2,1,0:T(2,128)}) %all-reduce.6.cloned.1.call-update) | async-done | bytes 102416 | tf_op jit(solution)/shard_map/psum | solution.py:120
  868.3 1.5 copy.107
  (65 shorter events, 18.6 us)
Async XLA Ops:
  7.2 176.2 %copy-start = (bf16[2,2,32,640]{3,2,1,0:T(8,128)(2,1)S(1)}, bf16[2,2,32,640]{3,2,1,0:T(8,128)(2,1)}, u32[]{:S(2)}) copy-start(bf16[2,2,32,640]{3,2,1,0:T(8,128)(2,1)} %param.11) | copy-start | bytes 491524
  7.2 37.8 %copy-start.4 = (bf16[2,2,32,640]{3,2,1,0:T(8,128)(2,1)S(1)}, bf16[2,2,32,640]{3,2,1,0:T(8,128)(2,1)}, u32[]{:S(2)}) copy-start(bf16[2,2,32,640]{3,2,1,0:T(8,128)(2,1)} %param.6) | copy-start | bytes 491524
  7.2 37.8 %copy-start.8 = (f32[640]{0:T(1024)S(1)}, f32[640]{0:T(1024)}, u32[]{:S(2)}) copy-start(f32[640]{0:T(1024)} %param.9) | copy-start | bytes 7684
  7.2 42.3 %copy-start.7 = (bf16[2,16,640]{2,1,0:T(8,128)(2,1)S(1)}, bf16[2,16,640]{2,1,0:T(8,128)(2,1)}, u32[]{:S(2)}) copy-start(bf16[2,16,640]{2,1,0:T(8,128)(2,1)} %param.7) | copy-start | bytes 122884
  7.2 157.2 %all-gather.5.cloned.1.call-start = ((), (), s32[]{:S(2)}) async-start(), calls=%async_computation.1 | async-start | bytes 3379200 | tf_op jit(solution)/shard_map/all_gather | solution.py:67
  7.9 390.9 %all-gather.3.cloned.1.call-start = ((), (), s32[]{:S(2)}) async-start(), calls=%async_computation | async-start | bytes 13516800 | tf_op jit(solution)/shard_map/all_gather | solution.py:61
  9.8 713.3 %all-reduce.8.cloned.1.call-start = ((), (), s32[]{:S(2)}) async-start(), calls=%async_computation.3 | async-start | bytes 6553600
  45.2 23.5 %collective-permute-start = (bf16[2,1,32,640]{3,2,1,0:T(8,128)(2,1)S(1)}, bf16[2,1,32,640]{3,2,1,0:T(8,128)(2,1)S(1)}, u32[]{:S(2)}, u32[]{:S(2)}) collective-permute-start(bf16[2,1,32,640]{3,2,1,0:T(8,128)(2,1)S(1)} %get-tuple-element.22), channel_id=1, source_target_pairs={{0,1},{1,2},{2,3},{3,4},{4,5},{5,6},{6,7},{7,8},{8,9},{9,10},{10,1... | collective-permute-start | bytes 245768 | tf_op jit(solution)/shard_map/ppermute | solution.py:20
  47.1 21.6 %collective-permute-start.1 = (bf16[2,1,32,640]{3,2,1,0:T(8,128)(2,1)S(1)}, bf16[2,1,32,640]{3,2,1,0:T(8,128)(2,1)S(1)}, u32[]{:S(2)}, u32[]{:S(2)}) collective-permute-start(bf16[2,1,32,640]{3,2,1,0:T(8,128)(2,1)S(1)} %get-tuple-element.23), channel_id=1, source_target_pairs={{1,0},{2,1},{3,2},{4,3},{5,4},{6,5},{7,6},{8,7},{9,8},{10,9},{11,1... | collective-permute-start | bytes 245768 | tf_op jit(solution)/shard_map/ppermute | solution.py:22
  398.8 8.4 copy-start.1
  406.6 0.7 copy-start.5
  406.6 2.1 copy-start.3
  435.5 289.1 %copy-start.2 = (bf16[128,640]{0,1:T(8,128)(2,1)S(1)}, bf16[128,640]{0,1:T(8,128)(2,1)}, u32[]{:S(2)}) copy-start(bf16[128,640]{0,1:T(8,128)(2,1)} %convert_element_type.72) | copy-start | bytes 491524
  435.5 289.1 %copy-start.6 = (bf16[128,640]{1,0:T(8,128)(2,1)S(1)}, bf16[128,640]{1,0:T(8,128)(2,1)}, u32[]{:S(2)}) copy-start(bf16[128,640]{1,0:T(8,128)(2,1)} %copy-done.5) | copy-start | bytes 491524
  435.5 432.8 %all-reduce.6.cloned.1.call-start = ((), (), s32[]{:S(2)}) async-start(), calls=%async_computation.2 | async-start | bytes 204800 | tf_op jit(solution)/shard_map/psum | solution.py:120
Sparse Core Ops, SparseCore 0:
  11.1 153.2 all-gather.4
  167.5 231.2 all-gather.2
  435.6 287.3 all-reduce.7
  726.4 141.8 all-reduce.5
where the time goes:
time: 877 us; the launch traced here: 876 us
  waiting for transfers between devices  732 us (83%)
  blocking collectives  52.6 us (6%)
  local copies, waits for them, and re-layouts  39.4 us (4%)
  matrix products  31.7 us (4%)
  between operations  14.7 us (2%)
    unnamed x5, waiting for transfers between devices  286 us
    all_gather x1, waiting for transfers between devices, body(): lax.all_gather(conv_weight, 'dp', axis=1, tiled=True)  213 us
    psum x1, waiting for transfers between devices, body(): weight_grads = lax.psum(own_rows, 'spatial')  143 us
    all_gather x1, waiting for transfers between devices, body(): weights = lax.all_gather(attn_weights, 'dp', axis=1, tiled=True)  89.4 us
    psum x1, blocking collectives, body(): first_sums, second_sums = lax.psum((first_sums, second_sums), 'spatial')  33.4 us
    all_gather x1, blocking collectives, body(): plan_all = lax.all_gather(plan, 'spatial', axis=1, tiled=True)  19.2 us
  transfers between devices with their start and end apart: 6, of which 4 were waited for; matrix products, arithmetic and copies ran while one was open for 4% of the time, Pallas kernels for 0%

commit v1 on v0

--- a/solution.py
+++ b/solution.py
@@ -7,6 +7,12 @@
 GROUPS = 32
 HEAD = 64
 eps_norm = 1e-05
+
+
+def summed_here(x, mesh_axis):
+    parts = lax.all_gather(x, mesh_axis, axis=0, tiled=False)
+    result = parts.sum(axis=0)
+    return result
 
 
 def with_halo(cells, sides, width):
@@ -117,7 +123,7 @@
     own_rows = lax.psum_scatter(
         jnp.stack([grad_query, grad_output], 1) * factor, "dp", scatter_dimension=0, tiled=True
     )
-    weight_grads = lax.psum(own_rows, "spatial")
+    weight_grads = summed_here(own_rows, "spatial")
     return (block_out, weight_grads)
 
 

time: 877 us -> 790 us (0.901)
  waiting for transfers between devices: 732 us -> 643 us
    psum x1 -> x0, waiting for transfers between devices: 143 us -> none  [body(): weight_grads = lax.psum(own_rows, 'spatial')]
    all_gather x0 -> x1, waiting for transfers between devices: none -> 54.4 us  [summed_here(): parts = lax.all_gather(x, mesh_axis, axis=0, tiled=False)]
where the time goes in v1:
time: 790 us; the launch traced here: 789 us
  waiting for transfers between devices  643 us (81%)
  blocking collectives  52.6 us (7%)
  local copies, waits for them, and re-layouts  37.9 us (5%)
  matrix products  31.7 us (4%)
  between operations  14.7 us (2%)
    unnamed x5, waiting for transfers between devices  286 us
    all_gather x1, waiting for transfers between devices, body(): lax.all_gather(conv_weight, 'dp', axis=1, tiled=True)  213 us
    all_gather x1, waiting for transfers between devices, body(): weights = lax.all_gather(attn_weights, 'dp', axis=1, tiled=True)  89.4 us
    all_gather x1, waiting for transfers between devices, summed_here(): parts = lax.all_gather(x, mesh_axis, axis=0, tiled=False)  54.4 us
    psum x1, blocking collectives, body(): first_sums, second_sums = lax.psum((first_sums, second_sums), 'spatial')  33.4 us
    all_gather x1, blocking collectives, body(): plan_all = lax.all_gather(plan, 'spatial', axis=1, tiled=True)  19.2 us
  transfers between devices with their start and end apart: 6, of which 4 were waited for; matrix products, arithmetic and copies ran while one was open for 4% of the time, Pallas kernels for 0%

profile of v1, /device:TPU:1, one launch (start us, length us, event | category | flops | bytes accessed | tf_op | source)
XLA Modules:
  0.0 789.2 jit_solution(6531288617233358421)
XLA Ops:
  8.0 1.8 copy.28
  11.2 33.4 %all-reduce.2 = (f32[2,32]{1,0:T(2,128)S(1)}, f32[2,32]{1,0:T(2,128)S(1)}) all-reduce(f32[2,32]{1,0:T(2,128)S(1)} %reduce_sum.64, f32[2,32]{1,0:T(2,128)S(1)} %reduce_sum.61), channel_id=1, replica_groups=mesh['dp'=32,'spatial'=16] {'spatial'}, use_global_device_ids=true, to_apply=%region_5.6 | all-reduce | flops 128 | bytes 1024 | tf_op jit(solution)/shard_map/psum | solution.py:44
  45.2 1.9 collective-permute-start
  47.1 2.4 collective-permute-start.1
  49.5 19.2 %all_gather.16 = bf16[2,256,640]{2,1,0:T(8,128)(2,1)S(1)} all-gather(bf16[2,16,640]{2,1,0:T(8,128)(2,1)S(1)} %copy-done.7), channel_id=1, replica_groups=mesh['dp'=32,'spatial'=16] {'spatial'}, dimensions={1}, use_global_device_ids=true | all-gather | bytes 696320 | tf_op jit(solution)/shard_map/all_gather | solution.py:79
  75.1 89.4 %all-gather.7.cloned.1.call-done = bf16[4,640,640]{2,0,1:T(4,128)(2,1)} async-done(((bf16[4,20,640]{2,0,1:T(4,128)(2,1)}), bf16[4,640,640]{2,0,1:T(4,128)(2,1)}) %all-gather.7.cloned.1.call-update) | async-done | bytes 3276816 | tf_op jit(solution)/shard_map/all_gather | solution.py:73
  164.4 12.3 %fusion.57 = (bf16[1,640,640]{2,0,1:T(2,128)(2,1)S(1)}, bf16[1,640,640]{2,0,1:T(2,128)(2,1)S(1)}, bf16[1,640,640]{2,0,1:T(2,128)(2,1)}, bf16[1,640,640]{2,0,1:T(2,128)(2,1)}) fusion(bf16[4,640,640]{2,0,1:T(4,128)(2,1)} %all-gather.7.cloned.1.call-done), kind=kLoop, calls=%fused_computation.73 | loop fusion | bytes 6553600 | tf_op jit(solution)/shard_map/slice | solution.py:77
  176.7 1.6 convolution_convert_fusion
  180.7 2.2 convolution_convert_fusion.1
  184.0 1.4 fusion.33
  185.4 213.4 %all-gather.5.cloned.1.call-done = bf16[9,640,640]{2,0,1:T(8,128)(2,1)} async-done(((bf16[9,20,640]{2,0,1:T(8,128)(2,1)}), bf16[9,640,640]{2,0,1:T(8,128)(2,1)}) %all-gather.5.cloned.1.call-update) | async-done | bytes 7372816 | tf_op jit(solution)/shard_map/all_gather | solution.py:67
  398.8 7.7 fusion.27
  408.7 2.6 fusion.60
  411.3 2.5 fusion.19
  413.8 9.3 %fusion.20 = bf16[2,64,10,64]{1,3,2,0:T(8,128)(2,1)S(1)} fusion(f32[2,10,64,256]{3,2,1,0:T(8,128)} %fusion.33, bf16[2,256,10,64]{1,0,3,2:T(2,128)(2,1)S(1)} %copy-done.3, f32[2,10,64,256]{3,2,1,0:T(8,128)} %get-tuple-element.23, f32[2,10,64]{2,1,0:T(8,128)S(1)} %get-tuple-element.22), kind=kOutput, calls=%fused_computation.25 | convolution fusion | flops 44320256 | bytes 3445760 | tf_op jit(solution)/shard_map/bhnm,bmhe->bnhe/dot_general | solution.py:116
  424.3 1.4 convolution_bitcast_fusion.1
  425.7 2.0 copy.39
  427.7 1.8 convert_element_type.72
  431.2 4.3 copy.46
  435.6 1.3 dynamic-slice
  437.6 285.5 %all-reduce.5.cloned.1.call-done = f32[640,2,640]{2,1,0:T(2,128)} async-done(((f32[640,2,640]{2,1,0:T(2,128)}), f32[640,2,640]{2,1,0:T(2,128)}) %all-reduce.5.cloned.1.call-update) | async-done | bytes 3276816
  723.1 1.5 constant_dynamic-slice_fusion
  725.7 54.4 %all-gather.9.cloned.1.call-done = f32[320,2,640]{2,1,0:T(2,128)} async-done(((f32[20,2,640]{2,1,0:T(2,128)}), f32[320,2,640]{2,1,0:T(2,128)}) %all-gather.9.cloned.1.call-update) | async-done | bytes 1638416 | tf_op jit(solution)/shard_map/all_gather | solution.py:13
  780.1 2.6 reduce_sum.67
  (65 shorter events, 18.6 us)
Async XLA Ops:
  7.2 176.2 %copy-start = (bf16[2,2,32,640]{3,2,1,0:T(8,128)(2,1)S(1)}, bf16[2,2,32,640]{3,2,1,0:T(8,128)(2,1)}, u32[]{:S(2)}) copy-start(bf16[2,2,32,640]{3,2,1,0:T(8,128)(2,1)} %param.11) | copy-start | bytes 491524
  7.2 37.8 %copy-start.4 = (bf16[2,2,32,640]{3,2,1,0:T(8,128)(2,1)S(1)}, bf16[2,2,32,640]{3,2,1,0:T(8,128)(2,1)}, u32[]{:S(2)}) copy-start(bf16[2,2,32,640]{3,2,1,0:T(8,128)(2,1)} %param.6) | copy-start | bytes 491524
  7.2 37.8 %copy-start.8 = (f32[640]{0:T(1024)S(1)}, f32[640]{0:T(1024)}, u32[]{:S(2)}) copy-start(f32[640]{0:T(1024)} %param.9) | copy-start | bytes 7684
  7.2 42.3 %copy-start.7 = (bf16[2,16,640]{2,1,0:T(8,128)(2,1)S(1)}, bf16[2,16,640]{2,1,0:T(8,128)(2,1)}, u32[]{:S(2)}) copy-start(bf16[2,16,640]{2,1,0:T(8,128)(2,1)} %param.7) | copy-start | bytes 122884
  7.2 157.2 %all-gather.7.cloned.1.call-start = ((), (), s32[]{:S(2)}) async-start(), calls=%async_computation.1 | async-start | bytes 3379200 | tf_op jit(solution)/shard_map/all_gather | solution.py:73
  7.9 390.9 %all-gather.5.cloned.1.call-start = ((), (), s32[]{:S(2)}) async-start(), calls=%async_computation | async-start | bytes 13516800 | tf_op jit(solution)/shard_map/all_gather | solution.py:67
  9.8 713.3 %all-reduce.5.cloned.1.call-start = ((), (), s32[]{:S(2)}) async-start(), calls=%async_computation.3 | async-start | bytes 6553600
  45.2 23.5 %collective-permute-start = (bf16[2,1,32,640]{3,2,1,0:T(8,128)(2,1)S(1)}, bf16[2,1,32,640]{3,2,1,0:T(8,128)(2,1)S(1)}, u32[]{:S(2)}, u32[]{:S(2)}) collective-permute-start(bf16[2,1,32,640]{3,2,1,0:T(8,128)(2,1)S(1)} %get-tuple-element.18), channel_id=1, source_target_pairs={{0,1},{1,2},{2,3},{3,4},{4,5},{5,6},{6,7},{7,8},{8,9},{9,10},{10,1... | collective-permute-start | bytes 245768 | tf_op jit(solution)/shard_map/ppermute | solution.py:26
  47.1 21.6 %collective-permute-start.1 = (bf16[2,1,32,640]{3,2,1,0:T(8,128)(2,1)S(1)}, bf16[2,1,32,640]{3,2,1,0:T(8,128)(2,1)S(1)}, u32[]{:S(2)}, u32[]{:S(2)}) collective-permute-start(bf16[2,1,32,640]{3,2,1,0:T(8,128)(2,1)S(1)} %get-tuple-element.19), channel_id=1, source_target_pairs={{1,0},{2,1},{3,2},{4,3},{5,4},{6,5},{7,6},{8,7},{9,8},{10,9},{11,1... | collective-permute-start | bytes 245768 | tf_op jit(solution)/shard_map/ppermute | solution.py:28
  398.8 8.4 %copy-start.1 = (bf16[1,640,640]{2,0,1:T(2,128)(2,1)S(1)}, bf16[1,640,640]{2,0,1:T(2,128)(2,1)}, u32[]{:S(2)}) copy-start(bf16[1,640,640]{2,0,1:T(2,128)(2,1)} %get-tuple-element.8) | copy-start | bytes 2457604
  406.6 0.7 copy-start.5
  406.6 2.1 copy-start.3
  435.5 289.1 %copy-start.2 = (bf16[128,640]{0,1:T(8,128)(2,1)S(1)}, bf16[128,640]{0,1:T(8,128)(2,1)}, u32[]{:S(2)}) copy-start(bf16[128,640]{0,1:T(8,128)(2,1)} %convert_element_type.72) | copy-start | bytes 491524
  435.5 289.1 %copy-start.6 = (bf16[128,640]{1,0:T(8,128)(2,1)S(1)}, bf16[128,640]{1,0:T(8,128)(2,1)}, u32[]{:S(2)}) copy-start(bf16[128,640]{1,0:T(8,128)(2,1)} %copy-done.5) | copy-start | bytes 491524
  435.5 344.6 %all-gather.9.cloned.1.call-start = ((), (), s32[]{:S(2)}) async-start(), calls=%async_computation.2 | async-start | bytes 1740800 | tf_op jit(solution)/shard_map/all_gather | solution.py:13
Sparse Core Ops, SparseCore 0:
  11.1 153.2 all-gather.6
  167.5 231.2 all-gather.4
  435.6 287.3 all-reduce.4
  725.6 54.4 all-gather.8
